TPU v7x, 32 devices: a whole 2x2x4 slice. The times are simulated.
32 devices in a mesh: row: 4 (over y, core), col: 8 (over z, x).
Axes of the slice: x: 2, y: 2, z: 4, core: 2. Of those that a mesh axis runs over, the one named last changes fastest.
Arguments:
- inverse: float32 [16384, 16384], P('row', 'col'), may hold values from -6 to 6
- front_blocks: int32 [2, 16], replicated, may hold values from 0 to 63, as said below
- panels: float32 [2, 4096, 256], P(None, 'row'), may hold values from -0.09375 to 0.09375
- diag_terms: float32 [2, 256, 256], replicated, may hold values from -6 to 6
- bounds: int32 [2, 4], replicated, may hold values from 1 to 128, 256 in all within a row
Outputs:
- border: float32 [2, 4096, 256], P(None, ('row', 'col'))
- diag_block: float32 [2, 256, 256], replicated
Inputs may be any that keep to these rules, and one draw needn't show every extreme that they name: `front_blocks`: each row names 16 distinct blocks. Positions 4 r to 4 r + 3 name blocks of four different groups of 16 consecutive blocks, and every such group is named at exactly four positions, of four different r. Positions 2 o and 2 o + 1 name blocks of two different groups of 8 consecutive blocks, and every such group is named at exactly two positions, of two different o.
All inputs are finite; a program needn't handle non-finite values.
Results may differ from a plain program's by a relative error of at most 0.0001.
Values sent between devices are 32-bit elements; how exact they have to be, the bound alone decides.
A program may use at most 128 MiB of HBM per device.

v0:
```python
import jax
import jax.numpy as jnp
from jax import lax
from jax.sharding import PartitionSpec as P

BS = 256


def body(inverse, front_blocks, panels, diag_terms, bounds):
    n_row = lax.axis_size("row")
    n_col = lax.axis_size("col")
    row_index = lax.axis_index("row")
    col_index = lax.axis_index("col")
    rows_loc, cols_loc = inverse.shape
    row_group = rows_loc // BS
    col_group = cols_loc // BS
    list_length = front_blocks.shape[1]
    per_owner = list_length // n_row
    highest = lax.Precision.HIGHEST
    borders = []
    diagonals = []
    for front_index in range(2):
        front_list = front_blocks[front_index]
        own_blocks = lax.dynamic_slice_in_dim(front_list, row_index * per_owner, per_owner)
        w_loc = panels[front_index]
        panel_width = w_loc.shape[1]
        w_pieces = w_loc.reshape(per_owner, BS, panel_width)
        targets = col_index * col_group + jnp.arange(col_group, dtype=jnp.int32)
        picker = (own_blocks[None, :] == targets[:, None]).astype(jnp.float32)
        own_piece = jnp.einsum("ki,iab->ab", picker, w_pieces, precision=highest)
        slot_rows = lax.all_gather(own_piece, "row", axis=0, tiled=True).reshape(
            n_row, BS, panel_width
        )
        owners = front_list.reshape(n_row, per_owner)
        placer = jnp.sum((owners[None, :, :] == targets[:, None, None]).astype(jnp.float32), axis=2)
        w_tilde = jnp.einsum("ks,sab->kab", placer, slot_rows, precision=highest).reshape(
            cols_loc, panel_width
        )
        dest_lists = front_list.reshape(n_row, per_owner)
        local_ids = row_index * row_group + jnp.arange(row_group, dtype=jnp.int32)
        share_rows = per_owner * BS // n_col
        full_rows = jnp.dot(inverse, w_tilde, precision=highest)
        quarters = BS // share_rows
        full_pieces = full_rows.reshape(row_group, quarters, share_rows, panel_width)
        first_rows = jnp.arange(n_col, dtype=jnp.int32) * share_rows
        dest_block = dest_lists[:, first_rows // BS]
        block_pick = (dest_block.T[:, :, None] == local_ids[None, None, :]).astype(jnp.float32)
        quarter_pick = (
            (first_rows % BS // share_rows)[:, None]
            == jnp.arange(quarters, dtype=jnp.int32)[None, :]
        ).astype(jnp.float32)
        sectioned = jnp.einsum("cq,kqap->ckap", quarter_pick, full_pieces, precision=highest)
        ordered = jnp.einsum("cdk,ckap->cdap", block_pick, sectioned, precision=highest)
        ordered = ordered.reshape(n_col * n_row * share_rows, panel_width)
        reduced = lax.psum_scatter(ordered, "col", scatter_dimension=0, tiled=True)
        received = lax.all_to_all(
            reduced.reshape(n_row, share_rows, panel_width),
            "row",
            split_axis=0,
            concat_axis=0,
            tiled=True,
        )
        product = jnp.sum(received, axis=0)
        w_mine = lax.dynamic_slice_in_dim(w_loc, col_index * share_rows, share_rows, 0)
        own_term = jnp.dot(w_mine.T, product, precision=highest)
        summed_total = lax.psum(own_term, ("row", "col"))
        node_ends = jnp.cumsum(bounds[front_index])
        columns = jnp.arange(panel_width, dtype=jnp.int32)
        node_ids = jnp.sum((columns[:, None] >= node_ends[None, :]).astype(jnp.int32), axis=1)
        same_node = (node_ids[:, None] == node_ids[None, :]).astype(jnp.float32)
        borders.append(-product)
        diagonals.append(same_node * (diag_terms[front_index] + summed_total))
    return (jnp.stack(borders), jnp.stack(diagonals))


def solution(mesh):
    placed = (P("row", "col"), P(), P(None, "row", None), P(), P())
    return jax.shard_map(
        body,
        mesh=mesh,
        in_specs=placed,
        out_specs=(P(None, ("row", "col"), None), P()),
        check_vma=False,
    )
```

profile of v0, /device:TPU:0, one launch (start us, length us, event | category | flops | bytes accessed | tf_op | source)
XLA Modules:
  0.0 484.4 jit_solution(6554460476007873666)
XLA Ops:
  7.2 0.0 all-gather.3.cloned.1.call-start
  7.2 0.8 slice_reduce_fusion.1
  8.0 1.7 fusion.46
  9.7 0.0 copy-start
  9.7 0.1 fusion.38
  9.8 0.2 convert_reduce_fusion.5
  10.0 2.3 fusion.6
  12.3 0.7 copy.51
  13.0 0.0 all-gather.3.cloned.1.call-update
  13.1 0.0 all-gather.5.cloned.1.call-start
  13.1 2.3 fusion.4
  15.5 0.7 copy.50
  16.2 0.0 all-gather.5.cloned.1.call-update
  16.2 0.0 reduce-scatter.3.cloned.1.call-start
  16.3 0.1 reshape_squeeze.12
  16.4 0.1 reshape_squeeze.14
  16.5 0.1 copy.17
  16.5 0.1 convert_reduce_fusion.1
  16.7 0.6 gather_fusion
  17.2 15.4 %all-gather.3.cloned.1.call-done = f32[1024,256]{1,0:T(8,128)} async-done(((f32[256,256]{1,0:T(8,128)}), f32[1024,256]{1,0:T(8,128)}) %all-gather.3.cloned.1.call-update) | async-done | bytes 1048592 | tf_op jit(solution)/shard_map/all_gather | solution.py:31
  32.6 4.0 fusion.10
  36.7 0.7 copy.19
  37.3 0.0 copy-done
  37.4 58.5 %convolution_bitcast_fusion.1 = f32[4096,256]{0,1:T(8,128)} fusion(f32[2048,256]{1,0:T(8,128)S(1)} %bitcast.104, f32[4096,2048]{1,0:T(8,128)} %param.5), kind=kOutput, calls=%fused_computation.7 | convolution fusion | flops 25769803776 | bytes 39845888 | tf_op jit(solution)/shard_map/dot_general | solution.py:42
  95.9 6.6 %reshape.215 = f32[16,2,128,256]{2,1,0,3:T(2,128)} reshape(f32[4096,256]{0,1:T(8,128)} %convolution_bitcast_fusion.1) | data formatting | bytes 8388608 | tf_op jit(solution)/shard_map/reshape | solution.py:44
  102.5 9.3 %copy.20 = f32[16,2,128,256]{3,1,2,0:T(2,128)} copy(f32[16,2,128,256]{2,1,0,3:T(2,128)} %reshape.215) | data formatting | bytes 8388608 | tf_op jit(solution)/shard_map/reshape | solution.py:44
  111.8 11.7 %fusion.34 = f32[8,16,128,256]{3,0,2,1:T(8,128)S(1)} fusion(f32[16,2,128,256]{3,1,2,0:T(2,128)} %copy.20, s32[8]{0:T(128)S(1)} %and_select_fusion), kind=kOutput, calls=%fused_computation.58 | convolution fusion | flops 100663312 | bytes 20971552 | tf_op jit(solution)/shard_map/cq,kqap->ckap/dot_general | solution.py:52
  123.5 12.2 %fusion.2 = f32[8,4,128,256]{3,1,2,0:T(4,128)S(1)} fusion(f32[8,16,128,256]{3,0,2,1:T(8,128)S(1)} %fusion.34, s32[16]{0:T(128)S(1)} %iota_add_fusion.1, s32[8,4]{1,0:T(8,128)S(1)} %gather_fusion), kind=kOutput, calls=%fused_computation.4 | convolution fusion | flops 201327104 | bytes 20971712 | tf_op jit(solution)/shard_map/cdk,ckap->cdap/dot_general | solution.py:53
  135.7 2.7 copy.22
  138.4 0.0 reduce-scatter.3.cloned.1.call-update
  138.4 0.0 reduce-scatter.5.cloned.1.call-start
  138.5 0.1 copy.23
  138.5 0.6 gather_fusion.1
  139.1 0.0 all-gather.5.cloned.1.call-done
  139.1 4.0 fusion.8
  143.2 0.7 copy.25
  143.8 58.8 %convolution_bitcast_fusion = f32[4096,256]{0,1:T(8,128)} fusion(f32[2048,256]{1,0:T(8,128)S(1)} %bitcast.105, f32[4096,2048]{1,0:T(8,128)} %param.5), kind=kOutput, calls=%fused_computation.6 | convolution fusion | flops 25769803776 | bytes 39845888 | tf_op jit(solution)/shard_map/dot_general | solution.py:42
  202.6 6.7 %reshape.220 = f32[16,2,128,256]{2,1,0,3:T(2,128)} reshape(f32[4096,256]{0,1:T(8,128)} %convolution_bitcast_fusion) | data formatting | bytes 8388608 | tf_op jit(solution)/shard_map/reshape | solution.py:44
  209.3 9.3 %copy.26 = f32[16,2,128,256]{3,1,2,0:T(2,128)} copy(f32[16,2,128,256]{2,1,0,3:T(2,128)} %reshape.220) | data formatting | bytes 8388608 | tf_op jit(solution)/shard_map/reshape | solution.py:44
  218.6 11.7 %fusion.32 = f32[8,16,128,256]{3,0,2,1:T(8,128)S(1)} fusion(f32[16,2,128,256]{3,1,2,0:T(2,128)} %copy.26, s32[8]{0:T(128)S(1)} %and_select_fusion), kind=kOutput, calls=%fused_computation.56 | convolution fusion | flops 100663312 | bytes 20971552 | tf_op jit(solution)/shard_map/cq,kqap->ckap/dot_general | solution.py:52
  230.3 12.2 %fusion = f32[8,4,128,256]{3,1,2,0:T(4,128)S(1)} fusion(f32[8,16,128,256]{3,0,2,1:T(8,128)S(1)} %fusion.32, s32[8,4]{1,0:T(8,128)S(1)} %gather_fusion.1, s32[16]{0:T(128)S(1)} %iota_add_fusion.1), kind=kOutput, calls=%fused_computation.2 | convolution fusion | flops 201327104 | bytes 20971712 | tf_op jit(solution)/shard_map/cdk,ckap->cdap/dot_general | solution.py:53
  242.5 2.7 copy.28
  245.2 0.0 copy-start.2
  245.2 0.0 copy-start.1
  245.2 0.0 reduce-scatter.5.cloned.1.call-update
  245.3 0.0 reduce-scatter.3.cloned.1.call-done
  245.3 3.6 all-to-all-start
  248.9 0.0 copy-done.2
  248.9 0.2 reduce-window.16
  249.1 0.2 reduce-window.17
  249.3 0.1 convert_reduce_fusion.2
  249.4 84.5 %reduce-scatter.5.cloned.1.call-done = f32[512,256]{1,0:T(8,128)} async-done(((f32[4096,256]{1,0:T(8,128)}), f32[512,256]{1,0:T(8,128)}) %reduce-scatter.5.cloned.1.call-update) | async-done | bytes 524304 | tf_op jit(solution)/shard_map/reduce_scatter | solution.py:55
  333.9 0.0 all-to-all-done
  333.9 3.5 all-to-all-start.1
  337.3 0.0 all-reduce.3.cloned.1.call-start
  337.5 2.1 fusion.18
  339.5 6.6 %all-to-all-done.1 = f32[4,128,256]{2,1,0:T(8,128)S(1)} async-done(((f32[4,128,256]{2,1,0:T(8,128)}), f32[4,128,256]{2,1,0:T(8,128)S(1)}, u32[]{:S(2)}, u32[]{:S(2)}) %all-to-all-start.1) | async-done | bytes 524320 | tf_op jit(solution)/shard_map/all_to_all | solution.py:56
  346.2 1.1 fusion.16
  347.3 0.0 all-reduce.3.cloned.1.call-update
  347.3 0.7 pad_maximum_fusion.1
  348.1 127.4 %all-reduce.3.cloned.1.call-done = (f32[256,256]{1,0:T(8,128)}, f32[256,256]{1,0:T(8,128)}) async-done(((f32[256,256]{1,0:T(8,128)}, f32[256,256]{1,0:T(8,128)}), (f32[256,256]{1,0:T(8,128)}, f32[256,256]{1,0:T(8,128)})) %all-reduce.3.cloned.1.call-update) | async-done | bytes 524304 | tf_op jit(solution)/shard_map/psum | solution.py:66
  475.5 0.0 copy-done.1
  475.5 1.2 fusion.15
  476.7 0.8 pad_maximum_fusion
  (10 shorter events, 0.1 us)
Async XLA Ops:
  7.2 25.5 %all-gather.3.cloned.1.call-start = ((), (), s32[]{:S(2)}) async-start(), calls=%async_computation.4 | async-start | bytes 1310720 | tf_op jit(solution)/shard_map/all_gather | solution.py:31
  9.7 27.7 %copy-start = (f32[1,1024,256]{2,1,0:T(8,128)}, f32[1,1024,256]{2,1,0:T(8,128)S(1)}, u32[]{:S(2)}) copy-start(f32[1,1024,256]{2,1,0:T(8,128)S(1)} %get-tuple-element.10) | copy-start | bytes 3145732
  13.1 126.1 %all-gather.5.cloned.1.call-start = ((), (), s32[]{:S(2)}) async-start(), calls=%async_computation.6 | async-start | bytes 1310720 | tf_op jit(solution)/shard_map/all_gather | solution.py:31
  16.2 229.1 %reduce-scatter.3.cloned.1.call-start = ((), (), s32[]{:S(2)}) async-start(), calls=%async_computation.5 | async-start | bytes 4718592 | tf_op jit(solution)/shard_map/reduce_scatter | solution.py:55
  138.4 195.5 %reduce-scatter.5.cloned.1.call-start = ((), (), s32[]{:S(2)}) async-start(), calls=%async_computation.7 | async-start | bytes 4718592 | tf_op jit(solution)/shard_map/reduce_scatter | solution.py:55
  245.2 3.7 copy-start.2
  245.2 230.3 %copy-start.1 = (f32[2,256,256]{2,1,0:T(8,128)S(1)}, f32[2,256,256]{2,1,0:T(8,128)}, u32[]{:S(2)}) copy-start(f32[2,256,256]{2,1,0:T(8,128)} %param.8) | copy-start | bytes 1572868
  245.3 88.6 %all-to-all-start = ((f32[4,128,256]{2,1,0:T(8,128)}), f32[4,128,256]{2,1,0:T(8,128)S(1)}, u32[]{:S(2)}, u32[]{:S(2)}) async-start(f32[4,128,256]{2,1,0:T(8,128)} %bitcast.112), calls=%async_computation.1 | async-start | bytes 1048576 | tf_op jit(solution)/shard_map/all_to_all | solution.py:56
  333.9 12.3 %all-to-all-start.1 = ((f32[4,128,256]{2,1,0:T(8,128)}), f32[4,128,256]{2,1,0:T(8,128)S(1)}, u32[]{:S(2)}, u32[]{:S(2)}) async-start(f32[4,128,256]{2,1,0:T(8,128)} %bitcast.113), calls=%async_computation.3 | async-start | bytes 1048576 | tf_op jit(solution)/shard_map/all_to_all | solution.py:56
  337.3 138.2 %all-reduce.3.cloned.1.call-start = ((), (), s32[]{:S(2)}) async-start(), calls=%async_computation.8 | async-start | bytes 1048576 | tf_op jit(solution)/shard_map/psum | solution.py:66
Sparse Core Ops, SparseCore 0:
  13.2 19.4 all-gather.2
  34.8 16.6 all-gather.4
  138.5 88.2 reduce-scatter.2
  245.4 88.4 reduce-scatter.4
  347.4 128.0 all-reduce.2
where the time goes:
time: 492 us; the launch traced here: 484 us
  waiting for transfers between devices  234 us (48%)
  matrix products  181 us (37%)
  local copies, waits for them, and re-layouts  44.1 us (9%)
  between operations  14.4 us (3%)
  starting transfers between devices  7.29 us (1%)
    psum x1, waiting for transfers between devices, body(): summed_total = lax.psum(own_term, ('row', 'col'))  127 us
    dot_general x2, matrix products, body(): full_rows = jnp.dot(inverse, w_tilde, precision=highest)  117 us
    reduce_scatter x2, waiting for transfers between devices, body(): reduced = lax.psum_scatter(ordered, 'col', scatter_dimension=0, tiled=True)  84.5 us
    reshape x4, local copies, waits for them, and re-layouts, body(): full_rows.reshape(row_group, quarters, share_rows, panel_width)  31.9 us
    dot_general x2, matrix products, body(): jnp.einsum('cdk,ckap->cdap', block_pick, sectioned, precision=highest)  24.4 us
    dot_general x2, matrix products, body(): jnp.einsum('cq,kqap->ckap', quarter_pick, full_pieces, precision=highest)  23.4 us
    all_gather x2, waiting for transfers between devices, body(): lax.all_gather(own_piece, 'row', axis=0, tiled=True)  15.4 us
  transfers between devices with their start and end apart: 7, of which 4 were waited for; matrix products, arithmetic and copies ran while one was open for 45% of the time, Pallas kernels for 0%

commit v1 on v0

--- a/solution.py
+++ b/solution.py
@@ -63,7 +63,7 @@
         product = jnp.sum(received, axis=0)
         w_mine = lax.dynamic_slice_in_dim(w_loc, col_index * share_rows, share_rows, 0)
         own_term = jnp.dot(w_mine.T, product, precision=highest)
-        summed_total = lax.psum(own_term, ("row", "col"))
+        summed_total = lax.psum(lax.psum(own_term, "col"), "row")
         node_ends = jnp.cumsum(bounds[front_index])
         columns = jnp.arange(panel_width, dtype=jnp.int32)
         node_ids = jnp.sum((columns[:, None] >= node_ends[None, :]).astype(jnp.int32), axis=1)

time: 492 us -> 471 us (0.957)
  waiting for transfers between devices: 234 us -> 212 us
    psum x1 -> x2, waiting for transfers between devices: 127 us -> 105 us  [body(): summed_total = lax.psum(lax.psum(own_term, 'col'), 'row')]
  transfers between devices with their start and end apart: 7 -> 8, of which waited for: 4 -> 5; matrix products, arithmetic and copies ran while one was open for 45% -> 47% of each run, Pallas kernels for 0% -> 0%
where the time goes in v1:
time: 471 us; the launch traced here: 463 us
  waiting for transfers between devices  212 us (45%)
  matrix products  181 us (38%)
  local copies, waits for them, and re-layouts  44.1 us (9%)
  between operations  14.7 us (3%)
  starting transfers between devices  7.33 us (2%)
    dot_general x2, matrix products, body(): full_rows = jnp.dot(inverse, w_tilde, precision=highest)  117 us
    psum x2, waiting for transfers between devices, body(): summed_total = lax.psum(lax.psum(own_term, 'col'), 'row')  105 us
    reduce_scatter x2, waiting for transfers between devices, body(): reduced = lax.psum_scatter(ordered, 'col', scatter_dimension=0, tiled=True)  85 us
    reshape x4, local copies, waits for them, and re-layouts, body(): full_rows.reshape(row_group, quarters, share_rows, panel_width)  31.9 us
    dot_general x2, matrix products, body(): jnp.einsum('cdk,ckap->cdap', block_pick, sectioned, precision=highest)  24.4 us
    dot_general x2, matrix products, body(): jnp.einsum('cq,kqap->ckap', quarter_pick, full_pieces, precision=highest)  23.4 us
    all_gather x2, waiting for transfers between devices, body(): lax.all_gather(own_piece, 'row', axis=0, tiled=True)  15.4 us
  transfers between devices with their start and end apart: 8, of which 5 were waited for; matrix products, arithmetic and copies ran while one was open for 47% of the time, Pallas kernels for 0%

profile of v1, /device:TPU:0, one launch (start us, length us, event | category | flops | bytes accessed | tf_op | source)
XLA Modules:
  0.0 463.2 jit_solution(5611014468856938280)
XLA Ops:
  7.2 0.0 all-gather.3.cloned.1.call-start
  7.2 0.8 slice_reduce_fusion.1
  8.0 1.7 fusion.46
  9.7 0.0 copy-start
  9.7 0.1 fusion.38
  9.8 0.2 convert_reduce_fusion.5
  10.0 2.3 fusion.6
  12.3 0.7 copy.51
  13.0 0.0 all-gather.3.cloned.1.call-update
  13.1 0.0 all-gather.5.cloned.1.call-start
  13.1 2.3 fusion.4
  15.5 0.7 copy.50
  16.2 0.0 all-gather.5.cloned.1.call-update
  16.2 0.0 reduce-scatter.3.cloned.1.call-start
  16.3 0.1 reshape_squeeze.12
  16.4 0.1 reshape_squeeze.14
  16.5 0.1 copy.17
  16.5 0.1 convert_reduce_fusion.1
  16.7 0.6 gather_fusion
  17.2 15.4 %all-gather.3.cloned.1.call-done = f32[1024,256]{1,0:T(8,128)} async-done(((f32[256,256]{1,0:T(8,128)}), f32[1024,256]{1,0:T(8,128)}) %all-gather.3.cloned.1.call-update) | async-done | bytes 1048592 | tf_op jit(solution)/shard_map/all_gather | solution.py:31
  32.6 4.0 fusion.10
  36.7 0.7 copy.19
  37.3 0.0 copy-done
  37.4 58.5 %convolution_bitcast_fusion.1 = f32[4096,256]{0,1:T(8,128)} fusion(f32[2048,256]{1,0:T(8,128)S(1)} %bitcast.104, f32[4096,2048]{1,0:T(8,128)} %param.5), kind=kOutput, calls=%fused_computation.7 | convolution fusion | flops 25769803776 | bytes 39845888 | tf_op jit(solution)/shard_map/dot_general | solution.py:42
  95.9 6.6 %reshape.215 = f32[16,2,128,256]{2,1,0,3:T(2,128)} reshape(f32[4096,256]{0,1:T(8,128)} %convolution_bitcast_fusion.1) | data formatting | bytes 8388608 | tf_op jit(solution)/shard_map/reshape | solution.py:44
  102.5 9.3 %copy.20 = f32[16,2,128,256]{3,1,2,0:T(2,128)} copy(f32[16,2,128,256]{2,1,0,3:T(2,128)} %reshape.215) | data formatting | bytes 8388608 | tf_op jit(solution)/shard_map/reshape | solution.py:44
  111.8 11.7 %fusion.34 = f32[8,16,128,256]{3,0,2,1:T(8,128)S(1)} fusion(f32[16,2,128,256]{3,1,2,0:T(2,128)} %copy.20, s32[8]{0:T(128)S(1)} %and_select_fusion), kind=kOutput, calls=%fused_computation.58 | convolution fusion | flops 100663312 | bytes 20971552 | tf_op jit(solution)/shard_map/cq,kqap->ckap/dot_general | solution.py:52
  123.5 12.2 %fusion.2 = f32[8,4,128,256]{3,1,2,0:T(4,128)S(1)} fusion(f32[8,16,128,256]{3,0,2,1:T(8,128)S(1)} %fusion.34, s32[16]{0:T(128)S(1)} %iota_add_fusion.1, s32[8,4]{1,0:T(8,128)S(1)} %gather_fusion), kind=kOutput, calls=%fused_computation.4 | convolution fusion | flops 201327104 | bytes 20971712 | tf_op jit(solution)/shard_map/cdk,ckap->cdap/dot_general | solution.py:53
  135.7 2.7 copy.22
  138.4 0.0 reduce-scatter.3.cloned.1.call-update
  138.4 0.0 reduce-scatter.5.cloned.1.call-start
  138.5 0.1 copy.23
  138.5 0.6 gather_fusion.1
  139.1 0.0 all-gather.5.cloned.1.call-done
  139.1 4.0 fusion.8
  143.2 0.7 copy.25
  143.8 58.8 %convolution_bitcast_fusion = f32[4096,256]{0,1:T(8,128)} fusion(f32[2048,256]{1,0:T(8,128)S(1)} %bitcast.105, f32[4096,2048]{1,0:T(8,128)} %param.5), kind=kOutput, calls=%fused_computation.6 | convolution fusion | flops 25769803776 | bytes 39845888 | tf_op jit(solution)/shard_map/dot_general | solution.py:42
  202.6 6.7 %reshape.220 = f32[16,2,128,256]{2,1,0,3:T(2,128)} reshape(f32[4096,256]{0,1:T(8,128)} %convolution_bitcast_fusion) | data formatting | bytes 8388608 | tf_op jit(solution)/shard_map/reshape | solution.py:44
  209.3 9.3 %copy.26 = f32[16,2,128,256]{3,1,2,0:T(2,128)} copy(f32[16,2,128,256]{2,1,0,3:T(2,128)} %reshape.220) | data formatting | bytes 8388608 | tf_op jit(solution)/shard_map/reshape | solution.py:44
  218.6 11.7 %fusion.32 = f32[8,16,128,256]{3,0,2,1:T(8,128)S(1)} fusion(f32[16,2,128,256]{3,1,2,0:T(2,128)} %copy.26, s32[8]{0:T(128)S(1)} %and_select_fusion), kind=kOutput, calls=%fused_computation.56 | convolution fusion | flops 100663312 | bytes 20971552 | tf_op jit(solution)/shard_map/cq,kqap->ckap/dot_general | solution.py:52
  230.3 12.2 %fusion = f32[8,4,128,256]{3,1,2,0:T(4,128)S(1)} fusion(f32[8,16,128,256]{3,0,2,1:T(8,128)S(1)} %fusion.32, s32[8,4]{1,0:T(8,128)S(1)} %gather_fusion.1, s32[16]{0:T(128)S(1)} %iota_add_fusion.1), kind=kOutput, calls=%fused_computation.2 | convolution fusion | flops 201327104 | bytes 20971712 | tf_op jit(solution)/shard_map/cdk,ckap->cdap/dot_general | solution.py:53
  242.5 2.7 copy.28
  245.2 0.0 reduce-scatter.5.cloned.1.call-update
  245.3 0.0 copy-start.1
  245.3 0.0 reduce-scatter.3.cloned.1.call-done
  245.3 3.6 all-to-all-start
  248.9 84.9 %reduce-scatter.5.cloned.1.call-done = f32[512,256]{1,0:T(8,128)} async-done(((f32[4096,256]{1,0:T(8,128)}), f32[512,256]{1,0:T(8,128)}) %reduce-scatter.5.cloned.1.call-update) | async-done | bytes 524304 | tf_op jit(solution)/shard_map/reduce_scatter | solution.py:55
  333.9 0.0 all-to-all-done
  333.9 3.5 all-to-all-start.1
  337.3 0.0 all-reduce.5.cloned.1.call-start
  337.4 2.0 fusion.18
  339.5 6.7 %all-to-all-done.1 = f32[4,128,256]{2,1,0:T(8,128)S(1)} async-done(((f32[4,128,256]{2,1,0:T(8,128)}), f32[4,128,256]{2,1,0:T(8,128)S(1)}, u32[]{:S(2)}, u32[]{:S(2)}) %all-to-all-start.1) | async-done | bytes 524320 | tf_op jit(solution)/shard_map/all_to_all | solution.py:56
  346.2 1.1 fusion.16
  347.3 0.0 all-reduce.5.cloned.1.call-update
  347.3 0.0 all-reduce.7.cloned.1.call-start
  347.4 0.2 reduce-window.16
  347.6 0.2 reduce-window.17
  347.7 0.1 convert_reduce_fusion.2
  347.8 71.1 %all-reduce.5.cloned.1.call-done = (f32[256,256]{1,0:T(8,128)}, f32[256,256]{1,0:T(8,128)}) async-done(((f32[256,256]{1,0:T(8,128)}, f32[256,256]{1,0:T(8,128)}), (f32[256,256]{1,0:T(8,128)}, f32[256,256]{1,0:T(8,128)})) %all-reduce.5.cloned.1.call-update) | async-done | bytes 524304 | tf_op jit(solution)/shard_map/psum | solution.py:66
  419.0 0.0 all-reduce.7.cloned.1.call-update
  419.0 0.7 pad_maximum_fusion.1
  419.7 34.2 %all-reduce.7.cloned.1.call-done = (f32[256,256]{1,0:T(8,128)}, f32[256,256]{1,0:T(8,128)}) async-done(((f32[256,256]{1,0:T(8,128)}, f32[256,256]{1,0:T(8,128)}), (f32[256,256]{1,0:T(8,128)}, f32[256,256]{1,0:T(8,128)})) %all-reduce.7.cloned.1.call-update) | async-done | bytes 524304 | tf_op jit(solution)/shard_map/psum | solution.py:66
  453.9 1.2 fusion.15
  455.1 0.8 pad_maximum_fusion
  (13 shorter events, 0.1 us)
Async XLA Ops:
  7.2 25.5 %all-gather.3.cloned.1.call-start = ((), (), s32[]{:S(2)}) async-start(), calls=%async_computation.4 | async-start | bytes 1310720 | tf_op jit(solution)/shard_map/all_gather | solution.py:31
  9.7 27.7 %copy-start = (f32[1,1024,256]{2,1,0:T(8,128)}, f32[1,1024,256]{2,1,0:T(8,128)S(1)}, u32[]{:S(2)}) copy-start(f32[1,1024,256]{2,1,0:T(8,128)S(1)} %get-tuple-element.12) | copy-start | bytes 3145732
  13.1 126.1 %all-gather.5.cloned.1.call-start = ((), (), s32[]{:S(2)}) async-start(), calls=%async_computation.6 | async-start | bytes 1310720 | tf_op jit(solution)/shard_map/all_gather | solution.py:31
  16.2 229.1 %reduce-scatter.3.cloned.1.call-start = ((), (), s32[]{:S(2)}) async-start(), calls=%async_computation.5 | async-start | bytes 4718592 | tf_op jit(solution)/shard_map/reduce_scatter | solution.py:55
  138.4 195.5 %reduce-scatter.5.cloned.1.call-start = ((), (), s32[]{:S(2)}) async-start(), calls=%async_computation.7 | async-start | bytes 4718592 | tf_op jit(solution)/shard_map/reduce_scatter | solution.py:55
  245.2 102.1 %copy-start.2 = (s32[2,4]{1,0:T(2,128)S(1)}, s32[2,4]{1,0:T(2,128)}, u32[]{:S(2)}) copy-start(s32[2,4]{1,0:T(2,128)} %param.9) | copy-start | bytes 100
  245.3 208.7 %copy-start.1 = (f32[2,256,256]{2,1,0:T(8,128)S(1)}, f32[2,256,256]{2,1,0:T(8,128)}, u32[]{:S(2)}) copy-start(f32[2,256,256]{2,1,0:T(8,128)} %param.8) | copy-start | bytes 1572868
  245.3 88.6 %all-to-all-start = ((f32[4,128,256]{2,1,0:T(8,128)}), f32[4,128,256]{2,1,0:T(8,128)S(1)}, u32[]{:S(2)}, u32[]{:S(2)}) async-start(f32[4,128,256]{2,1,0:T(8,128)} %bitcast.112), calls=%async_computation.1 | async-start | bytes 1048576 | tf_op jit(solution)/shard_map/all_to_all | solution.py:56
  333.9 12.3 %all-to-all-start.1 = ((f32[4,128,256]{2,1,0:T(8,128)}), f32[4,128,256]{2,1,0:T(8,128)S(1)}, u32[]{:S(2)}, u32[]{:S(2)}) async-start(f32[4,128,256]{2,1,0:T(8,128)} %bitcast.113), calls=%async_computation.3 | async-start | bytes 1048576 | tf_op jit(solution)/shard_map/all_to_all | solution.py:56
  337.3 81.6 %all-reduce.5.cloned.1.call-start = ((), (), s32[]{:S(2)}) async-start(), calls=%async_computation.8 | async-start | bytes 1048576 | tf_op jit(solution)/shard_map/psum | solution.py:66
  347.3 106.6 %all-reduce.7.cloned.1.call-start = ((), (), s32[]{:S(2)}) async-start(), calls=%async_computation.9 | async-start | bytes 1048576 | tf_op jit(solution)/shard_map/psum | solution.py:66
Sparse Core Ops, SparseCore 0:
  13.2 19.4 all-gather.2
  34.8 16.6 all-gather.4
  138.5 88.2 reduce-scatter.2
  245.4 88.4 reduce-scatter.4
  347.4 71.4 all-reduce.4
  421.2 32.6 all-reduce.6
